TPU v7x, 32 devices: a whole 2x2x4 slice. The times are simulated.
32 devices in a mesh: tbl: 8 (over z, core), grp: 4 (over y, x).
Axes of the slice: x: 2, y: 2, z: 4, core: 2. Of those that a mesh axis runs over, the one named last changes fastest.
Arguments:
- codes: bfloat16 [8, 1024, 256], P('tbl', 'grp'), may hold values from -4 to 4
- row_scales: float32 [8, 1024], P('tbl', 'grp'), may hold values from 0.25 to 16
- history_lengths: int32 [32, 8], P(None, 'tbl'), may hold values from 1 to 32, as said below
- history_ids: int32 [32, 8, 32], P(None, 'tbl'), may hold values from 0 to 1023, as said below
- query_items: int32 [32, 8], P(None, 'tbl'), may hold values from 0 to 1023, as said below
- slot_tables: int32 [8], replicated, may hold values from 0 to 7, each once
Outputs:
- pooled: bfloat16 [32, 8, 256], P(('tbl', 'grp'))
Inputs may be any that keep to these rules, and one draw needn't show every extreme that they name: `history_lengths`: the largest length, 32, occurs in every draw. `history_ids`: entries at positions at or beyond the history's length are row ids too, and are to be ignored. query_items[b, s] equals history_ids[b, s, h] for some h below history_lengths[b, s].
All inputs are finite; a program needn't handle non-finite values.
Results may differ from a plain program's by a relative error of at most 0.004.
Values may be sent and summed in bfloat16 or wider, within the bound.
A program may use at most 64 MiB of HBM per device.

v0:
```python
import jax
import jax.numpy as jnp
from jax import lax
from jax.sharding import PartitionSpec as P


def combined_all(value, axis, combine):
    everything = jax.tree.map(lambda part: lax.all_gather(part, axis), value)
    leading = jax.tree.map(lambda part: part[0], everything)

    def hop(k, so_far):
        return combine(so_far, jax.tree.map(lambda part: part[k], everything))

    return lax.fori_loop(1, lax.axis_size(axis), hop, leading)


def combine(first, second):
    first_peak, first_mass, first_sums = first
    second_peak, second_mass, second_sums = second
    peak = jnp.maximum(first_peak, second_peak)
    first_factor = jnp.exp(first_peak - peak)
    second_factor = jnp.exp(second_peak - peak)
    return (
        peak,
        first_mass * first_factor + second_mass * second_factor,
        first_sums * first_factor[..., None] + second_sums * second_factor[..., None],
    )


def per_device(codes, row_scales, history_lengths, history_ids, query_items, slot_tables):
    slot_count, row_count, emb_width = codes.shape
    batch_rows, _, history = history_ids.shape
    tbl_count = lax.axis_size("tbl")
    grp_count = lax.axis_size("grp")
    owned_rows = batch_rows // (tbl_count * grp_count)
    grp_index = lax.axis_index("grp")
    offset = grp_index * row_count
    query_local = query_items - offset
    query_owned = (query_local >= 0) & (query_local < row_count)
    query_index = jnp.clip(query_local, 0, row_count - 1)
    found = jnp.take(codes[0], query_index[:, 0], axis=0).astype(jnp.float32)
    factor = jnp.take(row_scales[0], query_index[:, 0], axis=0)
    code_parts = [jnp.where(query_owned[:, 0, None], found, 0.0)]
    scale_parts = [jnp.where(query_owned[:, 0], factor, 0.0)]
    query_codes = jnp.stack(code_parts, axis=1)
    query_scales = jnp.stack(scale_parts, axis=1)
    query = lax.psum((query_codes * query_scales[..., None]).astype(jnp.bfloat16), "grp").astype(
        jnp.float32
    )
    positions = jnp.arange(history, dtype=jnp.int32)
    row_iota = jnp.arange(row_count, dtype=jnp.int32)
    table_rows = codes.astype(jnp.float32)
    block_count = 8
    block_rows = batch_rows // block_count

    def partial_value(block):
        block_ids, block_lengths, block_query = block
        local = block_ids - offset
        live = positions[None, None, :] < block_lengths[:, :, None]
        local = jnp.where(live, local, -1)
        peaks, masses, sums = ([], [], [])
        rows_f = table_rows[0]
        factor = row_scales[0]
        counts = jnp.sum(
            (local[:, 0, :, None] == row_iota[None, None, :]).astype(jnp.float32), axis=1
        )
        raw = jnp.dot(block_query[:, 0], rows_f.T, precision=lax.Precision.HIGHEST)
        score = raw * factor[None, :] / emb_width
        named = counts > 0.0
        peak = jnp.max(jnp.where(named, score, -1e30), axis=1)
        weight = jnp.where(
            named,
            counts * jnp.exp(jnp.where(named, score, 0.0) - jnp.where(named, peak[:, None], 0.0)),
            0.0,
        )
        peaks.append(peak)
        masses.append(jnp.sum(weight, axis=1))
        sums.append(jnp.dot(weight * factor[None, :], rows_f, precision=lax.Precision.HIGHEST))
        return (jnp.stack(peaks, axis=1), jnp.stack(masses, axis=1), jnp.stack(sums, axis=1))

    block_peaks, block_masses, block_sums = lax.map(
        partial_value,
        (
            history_ids.reshape(block_count, block_rows, slot_count, history),
            history_lengths.reshape(block_count, block_rows, slot_count),
            query.reshape(block_count, block_rows, slot_count, emb_width),
        ),
    )
    lead = (tbl_count, grp_count, owned_rows)
    peaks = block_peaks.reshape(lead + (slot_count,))
    masses = block_masses.reshape(lead + (slot_count,))
    sums = block_sums.reshape(lead + (slot_count, emb_width))
    all_peak, all_mass, all_sums = combined_all((peaks, masses, sums), "grp", combine)
    mass = lax.dynamic_index_in_dim(all_mass, grp_index, 1, keepdims=False)
    weighted = lax.dynamic_index_in_dim(all_sums, grp_index, 1, keepdims=False)
    pooled_slot = (weighted / mass[..., None]).astype(jnp.bfloat16)
    outgoing = jnp.transpose(pooled_slot, (1, 0, 2, 3))
    arrived = lax.all_to_all(outgoing, "tbl", split_axis=1, concat_axis=1, tiled=True)
    arranged = arrived.reshape(owned_rows, tbl_count * slot_count, emb_width)
    inverse = jnp.argsort(slot_tables)
    return jnp.take(arranged, inverse, axis=1)


def solution(mesh):
    placed = (
        P("tbl", "grp", None),
        P("tbl", "grp"),
        P(None, "tbl"),
        P(None, "tbl", None),
        P(None, "tbl"),
        P(),
    )
    return jax.shard_map(
        per_device,
        mesh=mesh,
        in_specs=placed,
        out_specs=P(("tbl", "grp"), None, None),
        check_vma=False,
    )
```

profile of v0, /device:TPU:0, one launch (start us, length us, event | category | flops | bytes accessed | tf_op | source)
XLA Modules:
  0.0 74.8 jit_solution(50232354431573683)
XLA Ops:
  0.0 0.7 copy-done.2
  0.7 0.7 copy-done
  1.4 0.7 gather_fusion.1
  2.1 0.2 copy-done.1
  2.3 0.6 gather_fusion
  3.0 17.8 %psum.7 = bf16[8,4,1,256]{3,2,1,0:T(2,128)(2,1)S(1)} all-reduce(bf16[8,4,1,256]{3,2,1,0:T(2,128)(2,1)S(1)} %reshape.329), channel_id=1, replica_groups=mesh['tbl'=8,'grp'=4] {'grp'}, use_global_device_ids=true, to_apply=%region_1.2 | all-reduce | flops 8192 | bytes 32768 | tf_op jit(solution)/shard_map/psum | solution.py:47
  20.9 0.5 broadcast.216
  21.4 0.1 copy-done.3
  21.5 0.7 reduce.3
  22.3 14.2 %while.35 = (s32[]{:T(128)}, f32[8,4,1]{1,2,0:T(1,128)S(1)}, f32[8,4,1]{1,2,0:T(1,128)S(1)}, f32[8,4,1,256]{3,1,2,0:T(4,128)S(1)}, s32[8,4,1]{1,2,0:T(1,128)S(1)...) while((s32[]{:T(128)}, f32[8,4,1]{1,2,0:T(1,128)S(1)}, ...), condition=%wide.region_6.7_spmd.clone, body=%wide.region_2.6_spmd.clone.sunk | while | flops 6402426 | bytes 575205 | solution.py:81
  22.3 0.8 %bitcast_select_fusion.4 = s32[4,32]{1,0:T(4,128)S(1)} fusion(s32[8,4,1,32]{3,1,2,0:T(4,128)} %get-tuple-element.560, s32[]{:T(128)} %get-tuple-element.544, s32[]{:T(128)} %get-tuple-element.561, s32[4]{0:T(128)S(1)} %fusion.37), kind=kLoop, calls=%fused_computation.31.clone.1 | loop fusion | flops 384 | bytes 1048 | tf_op jit(solution)/shard_map/while/body/eval_jaxpr/jit(_where)/select_n | solution.py:60
  23.0 0.1 convert_reduce_fusion.2
  23.1 0.4 fusion.38
  23.6 0.2 fusion.39
  23.8 0.2 fusion.40
  24.0 0.8 %bitcast_select_fusion.4 = s32[4,32]{1,0:T(4,128)S(1)} fusion(s32[8,4,1,32]{3,1,2,0:T(4,128)} %get-tuple-element.560, s32[]{:T(128)} %get-tuple-element.544, s32[]{:T(128)} %get-tuple-element.561, s32[4]{0:T(128)S(1)} %fusion.37), kind=kLoop, calls=%fused_computation.31.clone.1 | loop fusion | flops 384 | bytes 1048 | tf_op jit(solution)/shard_map/while/body/eval_jaxpr/jit(_where)/select_n | solution.py:60
  24.8 0.1 convert_reduce_fusion.2
  24.9 0.4 fusion.38
  25.4 0.2 fusion.39
  25.5 0.2 fusion.40
  25.8 0.8 %bitcast_select_fusion.4 = s32[4,32]{1,0:T(4,128)S(1)} fusion(s32[8,4,1,32]{3,1,2,0:T(4,128)} %get-tuple-element.560, s32[]{:T(128)} %get-tuple-element.544, s32[]{:T(128)} %get-tuple-element.561, s32[4]{0:T(128)S(1)} %fusion.37), kind=kLoop, calls=%fused_computation.31.clone.1 | loop fusion | flops 384 | bytes 1048 | tf_op jit(solution)/shard_map/while/body/eval_jaxpr/jit(_where)/select_n | solution.py:60
  26.6 0.1 convert_reduce_fusion.2
  26.7 0.4 fusion.38
  27.1 0.2 fusion.39
  27.3 0.2 fusion.40
  27.6 0.8 %bitcast_select_fusion.4 = s32[4,32]{1,0:T(4,128)S(1)} fusion(s32[8,4,1,32]{3,1,2,0:T(4,128)} %get-tuple-element.560, s32[]{:T(128)} %get-tuple-element.544, s32[]{:T(128)} %get-tuple-element.561, s32[4]{0:T(128)S(1)} %fusion.37), kind=kLoop, calls=%fused_computation.31.clone.1 | loop fusion | flops 384 | bytes 1048 | tf_op jit(solution)/shard_map/while/body/eval_jaxpr/jit(_where)/select_n | solution.py:60
  28.4 0.1 convert_reduce_fusion.2
  28.5 0.4 fusion.38
  28.9 0.2 fusion.39
  29.1 0.2 fusion.40
  29.4 0.8 %bitcast_select_fusion.4 = s32[4,32]{1,0:T(4,128)S(1)} fusion(s32[8,4,1,32]{3,1,2,0:T(4,128)} %get-tuple-element.560, s32[]{:T(128)} %get-tuple-element.544, s32[]{:T(128)} %get-tuple-element.561, s32[4]{0:T(128)S(1)} %fusion.37), kind=kLoop, calls=%fused_computation.31.clone.1 | loop fusion | flops 384 | bytes 1048 | tf_op jit(solution)/shard_map/while/body/eval_jaxpr/jit(_where)/select_n | solution.py:60
  30.3 0.4 fusion.38
  30.7 0.2 fusion.39
  30.9 0.2 fusion.40
  31.2 0.8 %bitcast_select_fusion.4 = s32[4,32]{1,0:T(4,128)S(1)} fusion(s32[8,4,1,32]{3,1,2,0:T(4,128)} %get-tuple-element.560, s32[]{:T(128)} %get-tuple-element.544, s32[]{:T(128)} %get-tuple-element.561, s32[4]{0:T(128)S(1)} %fusion.37), kind=kLoop, calls=%fused_computation.31.clone.1 | loop fusion | flops 384 | bytes 1048 | tf_op jit(solution)/shard_map/while/body/eval_jaxpr/jit(_where)/select_n | solution.py:60
  31.9 0.1 convert_reduce_fusion.2
  32.1 0.4 fusion.38
  32.5 0.2 fusion.39
  32.7 0.2 fusion.40
  33.0 0.8 %bitcast_select_fusion.4 = s32[4,32]{1,0:T(4,128)S(1)} fusion(s32[8,4,1,32]{3,1,2,0:T(4,128)} %get-tuple-element.560, s32[]{:T(128)} %get-tuple-element.544, s32[]{:T(128)} %get-tuple-element.561, s32[4]{0:T(128)S(1)} %fusion.37), kind=kLoop, calls=%fused_computation.31.clone.1 | loop fusion | flops 384 | bytes 1048 | tf_op jit(solution)/shard_map/while/body/eval_jaxpr/jit(_where)/select_n | solution.py:60
  33.8 0.4 fusion.38
  34.3 0.2 fusion.39
  34.5 0.2 fusion.40
  34.7 0.8 %bitcast_select_fusion.4 = s32[4,32]{1,0:T(4,128)S(1)} fusion(s32[8,4,1,32]{3,1,2,0:T(4,128)} %get-tuple-element.560, s32[]{:T(128)} %get-tuple-element.544, s32[]{:T(128)} %get-tuple-element.561, s32[4]{0:T(128)S(1)} %fusion.37), kind=kLoop, calls=%fused_computation.31.clone.1 | loop fusion | flops 384 | bytes 1048 | tf_op jit(solution)/shard_map/while/body/eval_jaxpr/jit(_where)/select_n | solution.py:60
  35.5 0.1 convert_reduce_fusion.2
  35.6 0.4 fusion.38
  36.1 0.2 fusion.39
  36.3 0.2 fusion.40
  36.5 7.5 %all-gather.2 = f32[32,4,1,256]{3,1,2,0:T(4,128)S(1)} all-gather(f32[8,4,1,256]{3,1,2,0:T(4,128)S(1)} %get-tuple-element.250), channel_id=4, replica_groups=mesh['tbl'=8,'grp'=4] {'grp'}, dimensions={0}, use_global_device_ids=true | all-gather | bytes 163840 | tf_op jit(solution)/shard_map/all_gather | solution.py:8
  44.1 8.1 %all-gather = f32[32,4,1]{1,2,0:T(1,128)S(1)} all-gather(f32[8,4,1]{1,2,0:T(1,128)S(1)} %get-tuple-element.248), channel_id=2, replica_groups=mesh['tbl'=8,'grp'=4] {'grp'}, dimensions={0}, use_global_device_ids=true | all-gather | bytes 640 | tf_op jit(solution)/shard_map/all_gather | solution.py:8
  52.3 7.3 %all-gather.1 = f32[32,4,1]{1,2,0:T(1,128)S(1)} all-gather(f32[8,4,1]{1,2,0:T(1,128)S(1)} %get-tuple-element.249), channel_id=3, replica_groups=mesh['tbl'=8,'grp'=4] {'grp'}, dimensions={0}, use_global_device_ids=true | all-gather | bytes 640 | tf_op jit(solution)/shard_map/all_gather | solution.py:8
  59.8 1.4 %while.34 = (s32[]{:T(128)}, f32[8,4,1,1]{0,1,3,2:T(4,128)S(1)}, f32[8,4,1,1]{0,1,3,2:T(4,128)S(1)}, f32[8,4,1,1,256]{4,3,2,1,0:T(1,128)S(1)}, f32[4,8,4,1,1]{1,...) while((s32[]{:T(128)}, f32[8,4,1,1]{0,1,3,2:T(4,128)S(1)}, ...), condition=%wide.region_8.9_spmd, body=%wide.region_7.8_spmd.sunk | while | flops 24805 | bytes 166427 | solution.py:14
  60.0 0.2 fusion.34
  60.5 0.2 fusion.34
  61.0 0.2 fusion.34
  61.3 0.5 broadcast.218
  61.9 0.7 reduce.4
  62.5 0.6 reshape.339
  63.1 4.9 %all-to-all-start = ((bf16[8,2,128]{2,1,0:T(2,128)(2,1)}), bf16[8,2,128]{2,1,0:T(2,128)(2,1)S(1)}, u32[]{:S(2)}, u32[]{:S(2)}) async-start(bf16[8,2,128]{2,1,0:T(2,128)(2,1)} %reshape.339), calls=%async_computation | async-start | bytes 8192 | tf_op jit(solution)/shard_map/all_to_all | solution.py:98
  68.0 0.6 copy-done.4
  68.7 1.0 %sort.17 = (s32[8]{0:T(128)}, s32[8]{0:T(128)S(1)}) sort(s32[8]{0:T(128)S(1)} %copy-done.4, s32[8]{0:T(128)S(1)} %iota.10), dimensions={0}, to_apply=%region_0.1 | sort | flops 24 | bytes 128 | tf_op jit(solution)/shard_map/jit(argsort)/sort | solution.py:100
  69.7 3.8 %all-to-all-done = bf16[8,2,128]{2,1,0:T(2,128)(2,1)S(1)} async-done(((bf16[8,2,128]{2,1,0:T(2,128)(2,1)}), bf16[8,2,128]{2,1,0:T(2,128)(2,1)S(1)}, u32[]{:S(2)}, u32[]{:S(2)}) %all-to-all-start) | async-done | bytes 4128 | tf_op jit(solution)/shard_map/all_to_all | solution.py:98
  73.5 0.6 gather_fusion.2
  74.1 0.7 bitcast_select_fusion.2
  (76 shorter events, 2.0 us)
Async XLA Ops:
  0.0 0.7 copy-start.2
  0.7 0.7 copy-start
  1.4 0.9 %copy-start.1 = (bf16[1,256,256]{2,1,0:T(8,128)(2,1)S(1)}, bf16[1,256,256]{2,1,0:T(8,128)(2,1)}, u32[]{:S(2)}) copy-start(bf16[1,256,256]{2,1,0:T(8,128)(2,1)} %param.10) | copy-start | bytes 393220
  20.9 0.7 copy-start.3
  63.1 10.4 %all-to-all-start = ((bf16[8,2,128]{2,1,0:T(2,128)(2,1)}), bf16[8,2,128]{2,1,0:T(2,128)(2,1)S(1)}, u32[]{:S(2)}, u32[]{:S(2)}) async-start(bf16[8,2,128]{2,1,0:T(2,128)(2,1)} %reshape.339), calls=%async_computation | async-start | bytes 8192 | tf_op jit(solution)/shard_map/all_to_all | solution.py:98
  68.0 0.7 copy-start.4
where the time goes:
time: 75.3 us; the launch traced here: 74.8 us
  blocking collectives  40.7 us (54%)
  other arithmetic  12.5 us (17%)
  local copies, waits for them, and re-layouts  7.25 us (10%)
  matrix products  5.05 us (7%)
  starting transfers between devices  4.88 us (6%)
  waiting for transfers between devices  3.79 us (5%)
    all_gather x3, blocking collectives, combined_all(): everything = jax.tree.map(lambda part: lax.all_gather(part, axis), value)  22.9 us
    psum x1, blocking collectives, per_device(): lax.psum((query_codes * query_scales[..., None]).astype(jnp.bfloat16), 'g...  17.8 us
    select_n x8, other arithmetic, partial_value(): local = jnp.where(live, local, -1)  6.06 us
    all_to_all x1, starting transfers between devices, per_device(): lax.all_to_all(outgoing, 'tbl', split_axis=1, concat_axis=1, tiled=True)  4.88 us
    unnamed x15, local copies, waits for them, and re-layouts  3.95 us
    all_to_all x1, waiting for transfers between devices, per_device(): lax.all_to_all(outgoing, 'tbl', split_axis=1, concat_axis=1, tiled=True)  3.79 us
    dot_general x8, matrix products, partial_value(): raw = jnp.dot(block_query[:, 0], rows_f.T, precision=lax.Precision.HIGHEST)  3.42 us
    dot_general x8, matrix products, partial_value(): jnp.dot(weight * factor[None, :], rows_f, precision=lax.Precision.HIGHEST)  1.63 us
  transfers between devices with their start and end apart: 1, of which 1 were waited for; matrix products, arithmetic and copies ran while one was open for 1% of the time, Pallas kernels for 0%

commit v1 on v0

v1 whole, which is shorter than its diff:
```python
import functools

import jax
import jax.numpy as jnp
from jax import lax
from jax.experimental import pallas as pl
from jax.experimental.pallas import tpu as pltpu
from jax.sharding import PartitionSpec as P

LANES = 128
UNROLL = 64


def each(count, body):
    if count <= UNROLL:
        for k in range(1, count):
            body(k)
    else:
        lax.fori_loop(1, count, lambda k, c: (body(k), c)[1], 0)


def column(row):
    n = row.shape[1]
    same = lax.broadcasted_iota(jnp.int32, (n, n), 0) == lax.broadcasted_iota(jnp.int32, (n, n), 1)
    return jnp.sum(jnp.where(same, row, 0), axis=1, keepdims=True)


def kernel(
    tbl_n, grp_n, block,
    codes_hbm, scales_hbm, lengths_hbm, ids_hbm, items_hbm, tables_hbm,
    out_ref,
    codes, scales, lengths, ids, items, tables, query, query_in, counts, outbox, inbox,
    load_sem, table_sem, query_send, query_recv, send_sem, recv_sem,
):
    rows, emb = codes.shape
    batch, _, history = ids.shape
    owned = batch // (tbl_n * grp_n)
    n_dev = tbl_n * grp_n
    tbl_i = lax.axis_index("tbl")
    grp_i = lax.axis_index("grp")
    me = tbl_i * grp_n + grp_i

    loads = [
        pltpu.make_async_copy(src, dst, load_sem.at[i])
        for i, (src, dst) in enumerate(
            ((items_hbm, items), (codes_hbm, codes), (scales_hbm, scales),
             (lengths_hbm, lengths), (ids_hbm, ids))
        )
    ]
    for load in loads:
        load.start()
    table_load = pltpu.make_async_copy(tables_hbm, tables, table_sem)
    table_load.start()

    barrier = pltpu.get_barrier_semaphore()

    def greet(k):
        pl.semaphore_signal(
            barrier, inc=1, device_id=lax.rem(me + k, n_dev),
            device_id_type=pl.DeviceIdType.LOGICAL,
        )

    each(n_dev, greet)
    for load in loads:
        load.wait()

    row_scale = scales[...]
    offset = grp_i * rows
    lane_rows = lax.broadcasted_iota(jnp.int32, (block, rows), 1)
    lane = lax.broadcasted_iota(jnp.int32, (block, LANES), 1)
    blocks = [pl.ds(b * block, block) for b in range(batch // block)]

    for at in blocks:
        hit = column(items[:, at]) - offset == lane_rows
        found = jnp.dot(
            jnp.where(hit, 1.0, 0.0).astype(jnp.bfloat16), codes[...],
            preferred_element_type=jnp.float32,
        )
        factor = jnp.sum(jnp.where(hit, row_scale, 0.0), axis=1, keepdims=True)
        high = factor.astype(jnp.bfloat16).astype(jnp.float32)
        middle = (factor - high).astype(jnp.bfloat16).astype(jnp.float32)
        low = factor - high - middle
        query[at, :emb] = found.astype(jnp.bfloat16)
        query[at, emb:] = jnp.where(
            lane == 0, high, jnp.where(lane == 1, middle, jnp.where(lane == 2, low, 0.0))
        ).astype(jnp.bfloat16)

    pl.semaphore_wait(barrier, n_dev - 1)

    def ask(k):
        pltpu.make_async_remote_copy(
            src_ref=query, dst_ref=query_in.at[k - 1],
            send_sem=query_send, recv_sem=query_recv,
            device_id=tbl_i * grp_n + lax.rem(grp_i + k, grp_n),
            device_id_type=pl.DeviceIdType.LOGICAL,
        ).start()

    each(grp_n, ask)

    for at in blocks:
        local = ids[at, 0, :] - offset
        positions = lax.broadcasted_iota(jnp.int32, (block, history), 1)
        local = jnp.where(positions < column(lengths[:, at]), local, -1)
        total = jnp.zeros((block, rows), jnp.float32)
        for h in range(history):
            total += jnp.where(local[:, h:h + 1] == lane_rows, 1.0, 0.0)
        counts[at, :] = total

    arrived = pltpu.make_async_copy(query_in, query_in, query_recv)
    arrived.wait()

    for b, at in enumerate(blocks):
        asked = query[at, :]
        for k in range(grp_n - 1):
            asked += query_in[k, at, :]
        parts = asked[:, emb:].astype(jnp.float32)
        factor = parts[:, 0:1] + parts[:, 1:2] + parts[:, 2:3]
        raw = lax.dot_general(
            asked[:, :emb], codes[...], (((1,), (1,)), ((), ())),
            preferred_element_type=jnp.float32,
        )
        number = counts[at, :]
        score = jnp.where(number > 0.0, raw * factor * row_scale / emb, -1e30)
        peak = jnp.max(score, axis=1, keepdims=True)
        weight = number * jnp.exp(score - peak)
        mass = jnp.sum(weight, axis=1, keepdims=True)
        weight = weight * row_scale
        high = weight.astype(jnp.bfloat16)
        low = (weight - high.astype(jnp.float32)).astype(jnp.bfloat16)
        both = jnp.dot(
            jnp.concatenate([high, low], axis=0), codes[...],
            preferred_element_type=jnp.float32,
        )
        sums = both[:block] + both[block:]
        ends = jnp.where(lane == 0, peak, mass)
        for r in range(block):
            device, place = divmod(b * block + r, owned)
            outbox[device, place:place + 1, :emb] = sums[r:r + 1, :]
            outbox[device, place:place + 1, emb:] = ends[r:r + 1, :]

    slot = grp_i * tbl_n + tbl_i

    def give(k):
        target = lax.rem(me + k, n_dev)
        pltpu.make_async_remote_copy(
            src_ref=outbox.at[target], dst_ref=inbox.at[slot],
            send_sem=send_sem, recv_sem=recv_sem,
            device_id=target, device_id_type=pl.DeviceIdType.LOGICAL,
        ).start()

    each(n_dev, give)
    own = pltpu.make_async_copy(outbox.at[me], inbox.at[slot], recv_sem)
    own.start()
    table_load.wait()
    pltpu.make_async_copy(query_in, query_in, query_send).wait()
    pltpu.make_async_copy(inbox, inbox, recv_sem).wait()

    out_rows = lax.broadcasted_iota(jnp.int32, (tbl_n, emb), 0)
    for o in range(owned):
        shares = [inbox[pl.ds(g * tbl_n, tbl_n), o, :] for g in range(grp_n)]
        peak = shares[0][:, emb:emb + 1]
        for share in shares[1:]:
            peak = jnp.maximum(peak, share[:, emb:emb + 1])
        mass = jnp.zeros((tbl_n, 1), jnp.float32)
        sums = jnp.zeros((tbl_n, emb), jnp.float32)
        for share in shares:
            scale = jnp.exp(share[:, emb:emb + 1] - peak)
            mass += share[:, emb + 1:emb + 2] * scale
            sums += share[:, :emb] * scale
        pooled = sums / mass
        result = jnp.zeros((tbl_n, emb), jnp.float32)
        for s in range(tbl_n):
            result = jnp.where(out_rows == tables[s], pooled[s:s + 1, :], result)
        out_ref[o] = result.astype(jnp.bfloat16)
    sent = outbox.at[pl.ds(0, n_dev - 1)]
    pltpu.make_async_copy(sent, sent, send_sem).wait()


def per_device(tbl_n, grp_n, codes, row_scales, history_lengths, history_ids, query_items, slot_tables):
    _, rows, emb = codes.shape
    batch, _, history = history_ids.shape
    n_dev = tbl_n * grp_n
    owned = batch // n_dev
    block = min(32, batch)
    wide = emb + LANES
    hbm = pl.BlockSpec(memory_space=pl.ANY)
    return pl.pallas_call(
        functools.partial(kernel, tbl_n, grp_n, block),
        out_shape=jax.ShapeDtypeStruct((owned, tbl_n, emb), jnp.bfloat16),
        in_specs=[hbm] * 6,
        out_specs=pl.BlockSpec(memory_space=pltpu.VMEM),
        scratch_shapes=[
            pltpu.VMEM((rows, emb), codes.dtype),
            pltpu.VMEM((1, rows), jnp.float32),
            pltpu.VMEM((1, batch), jnp.int32),
            pltpu.VMEM((batch, 1, history), jnp.int32),
            pltpu.VMEM((1, batch), jnp.int32),
            pltpu.SMEM((tbl_n,), jnp.int32),
            pltpu.VMEM((batch, wide), jnp.bfloat16),
            pltpu.VMEM((grp_n - 1, batch, wide), jnp.bfloat16),
            pltpu.VMEM((batch, rows), jnp.float32),
            pltpu.VMEM((n_dev, owned, wide), jnp.float32),
            pltpu.VMEM((n_dev, owned, wide), jnp.float32),
            pltpu.SemaphoreType.DMA((5,)),
            pltpu.SemaphoreType.DMA,
            pltpu.SemaphoreType.DMA,
            pltpu.SemaphoreType.DMA,
            pltpu.SemaphoreType.DMA,
            pltpu.SemaphoreType.DMA,
        ],
        compiler_params=pltpu.CompilerParams(collective_id=0, has_side_effects=True),
    )(
        codes.reshape(rows, emb), row_scales, history_lengths.T, history_ids,
        query_items.T, slot_tables,
    )


def solution(mesh):
    placed = (
        P("tbl", "grp", None),
        P("tbl", "grp"),
        P(None, "tbl"),
        P(None, "tbl", None),
        P(None, "tbl"),
        P(),
    )
    return jax.shard_map(
        functools.partial(per_device, mesh.shape["tbl"], mesh.shape["grp"]),
        mesh=mesh,
        in_specs=placed,
        out_specs=P(("tbl", "grp"), None, None),
        check_vma=False,
    )
```

time: 75.3 us -> 16.7 us (0.22)
  blocking collectives: 40.7 us -> 0 us
  Pallas kernels: 0 us -> 15.3 us
  other arithmetic: 12.5 us -> 0 us
  local copies, waits for them, and re-layouts: 7.25 us -> 1.28 us
  matrix products: 5.05 us -> 0 us
  starting transfers between devices: 4.88 us -> 0 us
  waiting for transfers between devices: 3.79 us -> 0 us
    all_gather x3 -> x0, blocking collectives: 22.9 us -> none  [combined_all(): everything = jax.tree.map(lambda part: lax.all_gather(part, axis), value)]
    psum x1 -> x0, blocking collectives: 17.8 us -> none  [per_device(): lax.psum((query_codes * query_scales[..., None]).astype(jnp.bfloat16), 'g...]
    pallas_call x0 -> x1, Pallas kernels: none -> 15.3 us  [per_device(): pl.pallas_call(functools.partial(kernel, tbl_n, grp_n, block), out_shape=...]
    select_n x11 -> x0, other arithmetic: 6.74 us -> none  [the longest x8 6.06 us: partial_value(): local = jnp.where(live, local, -1)]
    dot_general x16 -> x0, matrix products: 5.05 us -> none  [the longest x8 3.42 us: partial_value(): raw = jnp.dot(block_query[:, 0], rows_f.T, precision=lax.Precision.HIGHEST)]
    all_to_all x1 -> x0, starting transfers between devices: 4.88 us -> none  [per_device(): lax.all_to_all(outgoing, 'tbl', split_axis=1, concat_axis=1, tiled=True)]
    all_to_all x1 -> x0, waiting for transfers between devices: 3.79 us -> none  [per_device(): lax.all_to_all(outgoing, 'tbl', split_axis=1, concat_axis=1, tiled=True)]
    unnamed x15 -> x1, local copies, waits for them, and re-layouts: 3.95 us -> 1.28 us
  transfers between devices with their start and end apart: 1 -> 0, of which waited for: 1 -> 0; matrix products, arithmetic and copies ran while one was open for 1% -> 0% of each run, Pallas kernels for 0% -> 0%
where the time goes in v1:
time: 16.7 us; the launch traced here: 16.6 us
  Pallas kernels  15.3 us (92%)
  local copies, waits for them, and re-layouts  1.28 us (8%)
    pallas_call x1, Pallas kernels, per_device(): pl.pallas_call(functools.partial(kernel, tbl_n, grp_n, block), out_shape=...  15.3 us
    unnamed x1, local copies, waits for them, and re-layouts  1.28 us

profile of v1, /device:TPU:0, one launch (start us, length us, event | category | flops | bytes accessed | tf_op | source)
XLA Modules:
  0.0 16.6 jit_solution(4002411429952820336)
XLA Ops:
  0.0 15.3 %shard_map.64 = bf16[1,8,256]{2,1,0:T(8,128)(2,1)} custom-call(bf16[256,256]{1,0:T(8,128)(2,1)} %bitcast.3, f32[1,256]{1,0:T(1,128)} %scales_hbm.1, s32[1,32]{1,0:T(1,128)} %bitcast.4, s32[32,1,32]{2,1,0:T(1,128)} %ids_hbm.1, s32[1,32]{1,0:T(1,128)} %bitcast.5, s32[8]{0:T(128)} %tables_hbm.1), custom_call_target="tpu_custom_call" | custom-call | tf_op jit(solution)/shard_map/pallas_call | solution.py:187
  15.3 1.3 %copy.8 = bf16[1,8,256]{2,1,0:T(8,128)(2,1)} copy(bf16[1,8,256]{2,1,0:T(8,128)(2,1)} %shard_map.64) | data formatting | bytes 8192

commit v2 on v1

--- a/solution.py
+++ b/solution.py
@@ -8,6 +8,7 @@
 from jax.sharding import PartitionSpec as P
 
 LANES = 128
+LOGICAL = pl.DeviceIdType.LOGICAL
 UNROLL = 64
 
 
@@ -29,8 +30,10 @@
     tbl_n, grp_n, block,
     codes_hbm, scales_hbm, lengths_hbm, ids_hbm, items_hbm, tables_hbm,
     out_ref,
-    codes, scales, lengths, ids, items, tables, query, query_in, counts, outbox, inbox,
-    load_sem, table_sem, query_send, query_recv, send_sem, recv_sem,
+    codes, scales, lengths, ids, items, tables, query, query_in, scales_in, factors, counts,
+    outbox, inbox,
+    load_sem, table_sem, query_send, query_recv, scales_send, scales_recv, send_sem, recv_sem,
+    ready,
 ):
     rows, emb = codes.shape
     batch, _, history = ids.shape
@@ -40,63 +43,67 @@
     grp_i = lax.axis_index("grp")
     me = tbl_i * grp_n + grp_i
 
+    pairs = (
+        (items_hbm, items), (codes_hbm, codes), (scales_hbm, scales),
+        (lengths_hbm, lengths), (ids_hbm, ids),
+    )
     loads = [
-        pltpu.make_async_copy(src, dst, load_sem.at[i])
-        for i, (src, dst) in enumerate(
-            ((items_hbm, items), (codes_hbm, codes), (scales_hbm, scales),
-             (lengths_hbm, lengths), (ids_hbm, ids))
-        )
+        pltpu.make_async_copy(src, dst, load_sem.at[i]) for i, (src, dst) in enumerate(pairs)
     ]
     for load in loads:
         load.start()
+    items_load, codes_load, scales_load, lengths_load, ids_load = loads
     table_load = pltpu.make_async_copy(tables_hbm, tables, table_sem)
     table_load.start()
 
     barrier = pltpu.get_barrier_semaphore()
 
-    def greet(k):
-        pl.semaphore_signal(
-            barrier, inc=1, device_id=lax.rem(me + k, n_dev),
-            device_id_type=pl.DeviceIdType.LOGICAL,
-        )
-
-    each(n_dev, greet)
-    for load in loads:
-        load.wait()
-
-    row_scale = scales[...]
+    tbl_bits = [1 << i for i in range(tbl_n.bit_length() - 1)]
+    grp_peers = [tbl_i * grp_n + lax.rem(grp_i + k, grp_n) for k in range(1, grp_n)]
+    tbl_peers = [lax.bitwise_xor(tbl_i, bit) * grp_n + grp_i for bit in tbl_bits]
+    for peer in grp_peers + tbl_peers:
+        pl.semaphore_signal(barrier, inc=1, device_id=peer, device_id_type=LOGICAL)
+
+    lane_rows = lax.broadcasted_iota(jnp.int32, (block, rows), 1)
+    blocks = [pl.ds(b * block, block) for b in range(batch // block)]
     offset = grp_i * rows
-    lane_rows = lax.broadcasted_iota(jnp.int32, (block, rows), 1)
-    lane = lax.broadcasted_iota(jnp.int32, (block, LANES), 1)
-    blocks = [pl.ds(b * block, block) for b in range(batch // block)]
-
+
+    items_load.wait()
+    codes_load.wait()
     for at in blocks:
         hit = column(items[:, at]) - offset == lane_rows
         found = jnp.dot(
             jnp.where(hit, 1.0, 0.0).astype(jnp.bfloat16), codes[...],
             preferred_element_type=jnp.float32,
         )
-        factor = jnp.sum(jnp.where(hit, row_scale, 0.0), axis=1, keepdims=True)
-        high = factor.astype(jnp.bfloat16).astype(jnp.float32)
-        middle = (factor - high).astype(jnp.bfloat16).astype(jnp.float32)
-        low = factor - high - middle
-        query[at, :emb] = found.astype(jnp.bfloat16)
-        query[at, emb:] = jnp.where(
-            lane == 0, high, jnp.where(lane == 1, middle, jnp.where(lane == 2, low, 0.0))
-        ).astype(jnp.bfloat16)
-
-    pl.semaphore_wait(barrier, n_dev - 1)
-
-    def ask(k):
+        query[at, :] = found.astype(jnp.bfloat16)
+    scales_load.wait()
+
+    pl.semaphore_wait(barrier, len(grp_peers) + len(tbl_peers))
+
+    for k, peer in enumerate(grp_peers):
         pltpu.make_async_remote_copy(
-            src_ref=query, dst_ref=query_in.at[k - 1],
+            src_ref=query, dst_ref=query_in.at[k],
             send_sem=query_send, recv_sem=query_recv,
-            device_id=tbl_i * grp_n + lax.rem(grp_i + k, grp_n),
-            device_id_type=pl.DeviceIdType.LOGICAL,
+            device_id=peer, device_id_type=LOGICAL,
         ).start()
-
-    each(grp_n, ask)
-
+    for k, peer in enumerate(grp_peers):
+        pltpu.make_async_remote_copy(
+            src_ref=scales, dst_ref=scales_in.at[k],
+            send_sem=scales_send, recv_sem=scales_recv,
+            device_id=peer, device_id_type=LOGICAL,
+        ).start()
+
+    def tell(i):
+        pl.semaphore_signal(
+            ready.at[i], inc=1, device_id=tbl_peers[i], device_id_type=LOGICAL
+        )
+
+    tell(0)
+    lengths_load.wait()
+    ids_load.wait()
+    row_scale = scales[...]
+    lane = lax.broadcasted_iota(jnp.int32, (block, LANES), 1)
     for at in blocks:
         local = ids[at, 0, :] - offset
         positions = lax.broadcasted_iota(jnp.int32, (block, history), 1)
@@ -106,17 +113,29 @@
             total += jnp.where(local[:, h:h + 1] == lane_rows, 1.0, 0.0)
         counts[at, :] = total
 
-    arrived = pltpu.make_async_copy(query_in, query_in, query_recv)
-    arrived.wait()
+    for i in range(len(tbl_bits)):
+        pl.semaphore_wait(ready.at[i], 1)
+        if i + 1 < len(tbl_bits):
+            tell(i + 1)
+
+    pltpu.make_async_copy(scales_in, scales_in, scales_recv).wait()
+    for at in blocks:
+        wanted = column(items[:, at])
+        total = jnp.where(wanted - offset == lane_rows, row_scale, 0.0)
+        for k in range(grp_n - 1):
+            theirs = lax.rem(grp_i + grp_n - 1 - k, grp_n) * rows
+            total += jnp.where(wanted - theirs == lane_rows, scales_in[k], 0.0)
+        factors[at, :] = jnp.sum(total, axis=1, keepdims=True)
+
+    pltpu.make_async_copy(query_in, query_in, query_recv).wait()
 
     for b, at in enumerate(blocks):
         asked = query[at, :]
         for k in range(grp_n - 1):
             asked += query_in[k, at, :]
-        parts = asked[:, emb:].astype(jnp.float32)
-        factor = parts[:, 0:1] + parts[:, 1:2] + parts[:, 2:3]
+        factor = factors[at, :]
         raw = lax.dot_general(
-            asked[:, :emb], codes[...], (((1,), (1,)), ((), ())),
+            asked, codes[...], (((1,), (1,)), ((), ())),
             preferred_element_type=jnp.float32,
         )
         number = counts[at, :]
@@ -145,7 +164,7 @@
         pltpu.make_async_remote_copy(
             src_ref=outbox.at[target], dst_ref=inbox.at[slot],
             send_sem=send_sem, recv_sem=recv_sem,
-            device_id=target, device_id_type=pl.DeviceIdType.LOGICAL,
+            device_id=target, device_id_type=LOGICAL,
         ).start()
 
     each(n_dev, give)
@@ -153,6 +172,7 @@
     own.start()
     table_load.wait()
     pltpu.make_async_copy(query_in, query_in, query_send).wait()
+    pltpu.make_async_copy(scales_in, scales_in, scales_send).wait()
     pltpu.make_async_copy(inbox, inbox, recv_sem).wait()
 
     out_rows = lax.broadcasted_iota(jnp.int32, (tbl_n, emb), 0)
@@ -176,6 +196,12 @@
     pltpu.make_async_copy(sent, sent, send_sem).wait()
 
 
+def store(pooled, out_hbm, sem):
+    out = pltpu.make_async_copy(pooled, out_hbm, sem)
+    out.start()
+    out.wait()
+
+
 def per_device(tbl_n, grp_n, codes, row_scales, history_lengths, history_ids, query_items, slot_tables):
     _, rows, emb = codes.shape
     batch, _, history = history_ids.shape
@@ -184,9 +210,9 @@
     block = min(32, batch)
     wide = emb + LANES
     hbm = pl.BlockSpec(memory_space=pl.ANY)
-    return pl.pallas_call(
+    pooled = pl.pallas_call(
         functools.partial(kernel, tbl_n, grp_n, block),
-        out_shape=jax.ShapeDtypeStruct((owned, tbl_n, emb), jnp.bfloat16),
+        out_shape=pltpu.VMEM((owned, tbl_n, emb), jnp.bfloat16),
         in_specs=[hbm] * 6,
         out_specs=pl.BlockSpec(memory_space=pltpu.VMEM),
         scratch_shapes=[
@@ -196,8 +222,10 @@
             pltpu.VMEM((batch, 1, history), jnp.int32),
             pltpu.VMEM((1, batch), jnp.int32),
             pltpu.SMEM((tbl_n,), jnp.int32),
-            pltpu.VMEM((batch, wide), jnp.bfloat16),
-            pltpu.VMEM((grp_n - 1, batch, wide), jnp.bfloat16),
+            pltpu.VMEM((batch, emb), jnp.bfloat16),
+            pltpu.VMEM((grp_n - 1, batch, emb), jnp.bfloat16),
+            pltpu.VMEM((grp_n - 1, 1, rows), jnp.float32),
+            pltpu.VMEM((batch, 1), jnp.float32),
             pltpu.VMEM((batch, rows), jnp.float32),
             pltpu.VMEM((n_dev, owned, wide), jnp.float32),
             pltpu.VMEM((n_dev, owned, wide), jnp.float32),
@@ -207,12 +235,22 @@
             pltpu.SemaphoreType.DMA,
             pltpu.SemaphoreType.DMA,
             pltpu.SemaphoreType.DMA,
+            pltpu.SemaphoreType.DMA,
+            pltpu.SemaphoreType.DMA,
+            pltpu.SemaphoreType.REGULAR((tbl_n.bit_length() - 1,)),
         ],
         compiler_params=pltpu.CompilerParams(collective_id=0, has_side_effects=True),
     )(
         codes.reshape(rows, emb), row_scales, history_lengths.T, history_ids,
         query_items.T, slot_tables,
     )
+    return pl.pallas_call(
+        store,
+        out_shape=jax.ShapeDtypeStruct((owned, tbl_n, emb), jnp.bfloat16),
+        in_specs=[pl.BlockSpec(memory_space=pltpu.VMEM)],
+        out_specs=pl.BlockSpec(memory_space=pl.ANY),
+        scratch_shapes=[pltpu.SemaphoreType.DMA],
+    )(pltpu.with_memory_space_constraint(pooled, pltpu.VMEM))
 
 
 def solution(mesh):

time: 16.7 us -> 15.1 us (0.904)
  local copies, waits for them, and re-layouts: 1.28 us -> 0 us
  Pallas kernels: 15.3 us -> 14.9 us
    unnamed x1 -> x0, local copies, waits for them, and re-layouts: 1.28 us -> none
    pallas_call x1, Pallas kernels: 15.3 us -> 14.3 us  [per_device(): pl.pallas_call(functools.partial(kernel, tbl_n, grp_n, block), out_shape=...]
    pallas_call x0 -> x1, Pallas kernels: none -> 0.6 us  [per_device(): pl.pallas_call(store, out_shape=jax.ShapeDtypeStruct((owned, tbl_n, emb),...]
where the time goes in v2:
time: 15.1 us; the launch traced here: 15 us
  Pallas kernels  14.9 us (99%)
    pallas_call x1, Pallas kernels, per_device(): pl.pallas_call(functools.partial(kernel, tbl_n, grp_n, block), out_shape=...  14.3 us
    pallas_call x1, Pallas kernels, per_device(): pl.pallas_call(store, out_shape=jax.ShapeDtypeStruct((owned, tbl_n, emb),...  0.6 us

profile of v2, /device:TPU:0, one launch (start us, length us, event | category | flops | bytes accessed | tf_op | source)
XLA Modules:
  0.0 15.0 jit_solution(10215527372425800135)
XLA Ops:
  0.0 14.3 %shard_map.64.pooled = bf16[1,8,256]{2,1,0:T(8,128)(2,1)S(1)} custom-call(bf16[256,256]{1,0:T(8,128)(2,1)} %bitcast.3, f32[1,256]{1,0:T(1,128)} %scales_hbm.1, s32[1,32]{1,0:T(1,128)} %bitcast.4, s32[32,1,32]{2,1,0:T(1,128)} %ids_hbm.1, s32[1,32]{1,0:T(1,128)} %bitcast.5, s32[8]{0:T(128)} %tables_hbm.1), custom_call_target="tpu_custom_call" | custom-call | tf_op jit(solution)/shard_map/pallas_call | solution.py:213
  14.3 0.6 %shard_map.65 = bf16[1,8,256]{2,1,0:T(8,128)(2,1)} custom-call(bf16[1,8,256]{2,1,0:T(8,128)(2,1)S(1)} %shard_map.64.pooled), custom_call_target="tpu_custom_call" | custom-call | tf_op jit(solution)/shard_map/pallas_call | solution.py:247

commit v3 on v2

--- a/solution.py
+++ b/solution.py
@@ -81,12 +81,14 @@
 
     pl.semaphore_wait(barrier, len(grp_peers) + len(tbl_peers))
 
-    for k, peer in enumerate(grp_peers):
-        pltpu.make_async_remote_copy(
-            src_ref=query, dst_ref=query_in.at[k],
-            send_sem=query_send, recv_sem=query_recv,
-            device_id=peer, device_id_type=LOGICAL,
-        ).start()
+    for half in range(2):
+        part = pl.ds(half * (batch // 2), batch // 2)
+        for k, peer in enumerate(grp_peers):
+            pltpu.make_async_remote_copy(
+                src_ref=query.at[part], dst_ref=query_in.at[half, k],
+                send_sem=query_send, recv_sem=query_recv.at[half],
+                device_id=peer, device_id_type=LOGICAL,
+            ).start()
     for k, peer in enumerate(grp_peers):
         pltpu.make_async_remote_copy(
             src_ref=scales, dst_ref=scales_in.at[k],
@@ -127,12 +129,26 @@
             total += jnp.where(wanted - theirs == lane_rows, scales_in[k], 0.0)
         factors[at, :] = jnp.sum(total, axis=1, keepdims=True)
 
-    pltpu.make_async_copy(query_in, query_in, query_recv).wait()
-
+    slot = grp_i * tbl_n + tbl_i
+
+    def give(target):
+        @pl.when(target != me)
+        def _():
+            pltpu.make_async_remote_copy(
+                src_ref=outbox.at[target], dst_ref=inbox.at[slot],
+                send_sem=send_sem, recv_sem=recv_sem,
+                device_id=target, device_id_type=LOGICAL,
+            ).start()
+
+    per_half = len(blocks) // 2
     for b, at in enumerate(blocks):
+        half, inner = divmod(b, per_half)
+        if inner == 0:
+            landed = query_in.at[half]
+            pltpu.make_async_copy(landed, landed, query_recv.at[half]).wait()
         asked = query[at, :]
         for k in range(grp_n - 1):
-            asked += query_in[k, at, :]
+            asked += query_in[half, k, pl.ds(inner * block, block), :]
         factor = factors[at, :]
         raw = lax.dot_general(
             asked, codes[...], (((1,), (1,)), ((), ())),
@@ -157,17 +173,13 @@
             outbox[device, place:place + 1, :emb] = sums[r:r + 1, :]
             outbox[device, place:place + 1, emb:] = ends[r:r + 1, :]
 
-    slot = grp_i * tbl_n + tbl_i
-
-    def give(k):
-        target = lax.rem(me + k, n_dev)
-        pltpu.make_async_remote_copy(
-            src_ref=outbox.at[target], dst_ref=inbox.at[slot],
-            send_sem=send_sem, recv_sem=recv_sem,
-            device_id=target, device_id_type=LOGICAL,
-        ).start()
-
-    each(n_dev, give)
+        if inner == per_half - 1:
+            for k in range(n_dev // 2) if n_dev <= UNROLL else ():
+                give(half * (n_dev // 2) + k)
+            if n_dev > UNROLL:
+                first = half * (n_dev // 2)
+                lax.fori_loop(first, first + n_dev // 2, lambda t, c: (give(t), c)[1], 0)
+
     own = pltpu.make_async_copy(outbox.at[me], inbox.at[slot], recv_sem)
     own.start()
     table_load.wait()
@@ -207,7 +219,7 @@
     batch, _, history = history_ids.shape
     n_dev = tbl_n * grp_n
     owned = batch // n_dev
-    block = min(32, batch)
+    block = min(32, batch // 2)
     wide = emb + LANES
     hbm = pl.BlockSpec(memory_space=pl.ANY)
     pooled = pl.pallas_call(
@@ -223,7 +235,7 @@
             pltpu.VMEM((1, batch), jnp.int32),
             pltpu.SMEM((tbl_n,), jnp.int32),
             pltpu.VMEM((batch, emb), jnp.bfloat16),
-            pltpu.VMEM((grp_n - 1, batch, emb), jnp.bfloat16),
+            pltpu.VMEM((2, grp_n - 1, batch // 2, emb), jnp.bfloat16),
             pltpu.VMEM((grp_n - 1, 1, rows), jnp.float32),
             pltpu.VMEM((batch, 1), jnp.float32),
             pltpu.VMEM((batch, rows), jnp.float32),
@@ -232,7 +244,7 @@
             pltpu.SemaphoreType.DMA((5,)),
             pltpu.SemaphoreType.DMA,
             pltpu.SemaphoreType.DMA,
-            pltpu.SemaphoreType.DMA,
+            pltpu.SemaphoreType.DMA((2,)),
             pltpu.SemaphoreType.DMA,
             pltpu.SemaphoreType.DMA,
             pltpu.SemaphoreType.DMA,

time: 15.1 us -> 15.1 us (level)
  no operation moved by 1% of the time
where the time goes in v3:
time: 15.1 us; the launch traced here: 15 us
  Pallas kernels  15 us (99%)
    pallas_call x1, Pallas kernels, per_device(): pl.pallas_call(functools.partial(kernel, tbl_n, grp_n, block), out_shape=...  14.4 us
    pallas_call x1, Pallas kernels, per_device(): pl.pallas_call(store, out_shape=jax.ShapeDtypeStruct((owned, tbl_n, emb),...  0.6 us

profile of v3, /device:TPU:0, one launch (start us, length us, event | category | flops | bytes accessed | tf_op | source)
XLA Modules:
  0.0 15.0 jit_solution(3918790696649031145)
XLA Ops:
  0.0 14.4 %shard_map.64.pooled = bf16[1,8,256]{2,1,0:T(8,128)(2,1)S(1)} custom-call(bf16[256,256]{1,0:T(8,128)(2,1)} %bitcast.3, f32[1,256]{1,0:T(1,128)} %scales_hbm.1, s32[1,32]{1,0:T(1,128)} %bitcast.4, s32[32,1,32]{2,1,0:T(1,128)} %ids_hbm.1, s32[1,32]{1,0:T(1,128)} %bitcast.5, s32[8]{0:T(128)} %tables_hbm.1), custom_call_target="tpu_custom_call" | custom-call | tf_op jit(solution)/shard_map/pallas_call | solution.py:225
  14.4 0.6 %shard_map.65 = bf16[1,8,256]{2,1,0:T(8,128)(2,1)} custom-call(bf16[1,8,256]{2,1,0:T(8,128)(2,1)S(1)} %shard_map.64.pooled), custom_call_target="tpu_custom_call" | custom-call | tf_op jit(solution)/shard_map/pallas_call | solution.py:259
